TPU v7x, 256 devices: a whole 4x4x8 slice. The times are simulated.
256 devices in a mesh: row: 8 (over x, core), col: 32 (over y, z).
Axes of the slice: x: 4, y: 4, z: 8, core: 2. Of those that a mesh axis runs over, the one named last changes fastest.
Arguments:
- connectivity: int32 [4, 2097152], P(None, ('row', 'col')), may hold values from 0 to 3071
- gradients: float32 [9, 2097152], P(None, ('row', 'col')), may hold values from -4 to 4
- volumes: float32 [2097152], P(('row', 'col')), may hold values from 0.2 to 1
- live_blocks: int32 [256], P(('row', 'col')), may hold values from 1 to 8, as said below
- send_lists: int32 [4, 65536], P(None, ('row', 'col')), may hold values from 0 to 2047
- divergence: float32 [524288], P(('row', 'col')), may hold values from -6 to 6
- mass_shift: float32 [524288], P(('row', 'col')), may hold values from 0.5 to 4
- boundary_nodes: int32 [81920], P(('row', 'col')), may hold values from 0 to 2047
- surface_points: float32 [3, 81920], P(None, ('row', 'col')), may hold values from 0 to 1
- normal_cos: float32 [81920], P(('row', 'col')), may hold values from -1 to 1
- normal_angle: float32 [81920], P(('row', 'col')), may hold values from -3.140625 to 3.140625
- node_areas: float32 [81920], P(('row', 'col')), may hold values from 0.00036621094 to 0.0014648438
Outputs:
- potential: float32 [524288], P(('row', 'col'))
- dirichlet: float32 [8192], P(('row', 'col'))
Inputs may be any that keep to these rules, and one draw needn't show every extreme that they name: The first live_blocks[p] element blocks of partition p are live, the rest are padding; some partition has all 8 blocks live. `connectivity`: indices into the partition's extended node list. `send_lists`: indices of the partition's own nodes. `boundary_nodes`: indices of the partition's own nodes.
All inputs are finite; a program needn't handle non-finite values.
Results may differ from a plain program's by a relative error of at most 0.0024.
Values sent between devices are 32-bit elements; how exact they have to be, the bound alone decides.
No kernel may reach another device: no remote copies, remote signals or barrier semaphores. Data moves between devices by JAX's collectives and lax.ppermute only.
A program may use at most 64 MiB of HBM per device.

v0:
```python
import math
import jax
import jax.numpy as jnp
from jax import lax
from jax.sharding import PartitionSpec as P

TGT_DEV = 32
NBLK = 8
ITERS = 3
smoothing = 0.0001
inverse_four_pi = 1.0 / (4.0 * math.pi)


def with_halo(block, sides, width):
    for axis, dim in sides:
        count = lax.axis_size(axis)
        forward = [(i, i + 1) for i in range(count - 1)]
        backward = [(target, source) for source, target in forward]
        low = lax.ppermute(
            lax.slice_in_dim(block, block.shape[dim] - width, None, axis=dim), axis, forward
        )
        high = lax.ppermute(lax.slice_in_dim(block, 0, width, axis=dim), axis, backward)
        block = jnp.concatenate([low, block, high], axis=dim)
    return block


def pick_block(total, largest):
    for candidate in range(min(total, largest), 0, -1):
        if total % candidate == 0:
            return candidate
    return 1


def element_terms(extended, corners, gradients, volumes):
    corner_values = extended[corners]
    grad_zero = gradients[0:3]
    grad_one = gradients[3:6]
    grad_two = gradients[6:9]
    grad_three = -(grad_zero + grad_one + grad_two)
    field_grad = (
        grad_zero * corner_values[0]
        + grad_one * corner_values[1]
        + grad_two * corner_values[2]
        + grad_three * corner_values[3]
    )
    return (
        jnp.stack(
            [
                jnp.sum(gradient * field_grad, axis=0)
                for gradient in (grad_zero, grad_one, grad_two, grad_three)
            ]
        )
        * volumes
    )


def kernel_rows(targets, sources):
    delta_x = targets[0][:, None] - sources[0][None, :]
    delta_y = targets[1][:, None] - sources[1][None, :]
    delta_z = targets[2][:, None] - sources[2][None, :]
    radius_sq = delta_x * delta_x + delta_y * delta_y + delta_z * delta_z + smoothing
    inverse = lax.rsqrt(radius_sq)
    numerator = (
        delta_x * sources[3][None, :]
        + delta_y * sources[4][None, :]
        + delta_z * sources[5][None, :]
    )
    entries = (numerator * (inverse * inverse * inverse) * inverse_four_pi).astype(jnp.bfloat16)
    return jnp.dot(entries, sources[6].astype(jnp.bfloat16), preferred_element_type=jnp.float32)


def fetch_ghosts(values, send_lists):
    picked = values[send_lists]
    empty = jnp.zeros_like(picked[0])
    layout = jnp.stack(
        [
            jnp.stack([empty, picked[1], empty]),
            jnp.stack([picked[3], empty, picked[2]]),
            jnp.stack([empty, picked[0], empty]),
        ]
    )
    extended = with_halo(layout, (("row", 0), ("col", 1)), 1)
    return jnp.concatenate([extended[0, 2], extended[4, 2], extended[2, 0], extended[2, 4]])


def return_ghosts(ghost_terms):
    empty = jnp.zeros_like(ghost_terms[0])
    layout = jnp.stack(
        [
            jnp.stack([empty, ghost_terms[0], empty]),
            jnp.stack([ghost_terms[2], empty, ghost_terms[3]]),
            jnp.stack([empty, ghost_terms[1], empty]),
        ]
    )
    extended = with_halo(layout, (("row", 0), ("col", 1)), 1)
    return jnp.stack([extended[4, 2], extended[0, 2], extended[2, 4], extended[2, 0]])


def apply_operator(values, connectivity, gradients, volumes, live_blocks, send_lists, mass_shift):
    nodes = values.shape[0]
    extended = jnp.concatenate([values, fetch_ghosts(values, send_lists)])
    block_size = connectivity.shape[1] // NBLK

    def add_block(block_index, total):
        start = block_index * block_size
        corners = lax.dynamic_slice_in_dim(connectivity, start, block_size, 1)
        block_grads = lax.dynamic_slice_in_dim(gradients, start, block_size, 1)
        block_volumes = lax.dynamic_slice_in_dim(volumes, start, block_size, 0)
        return total.at[corners].add(element_terms(extended, corners, block_grads, block_volumes))

    assembled = lax.fori_loop(0, live_blocks[0], add_block, jnp.zeros(extended.shape, jnp.float32))
    owned = assembled[:nodes]
    ghost_terms = assembled[nodes:].reshape(4, -1)
    owned = owned.at[send_lists].add(return_ghosts(ghost_terms))
    return mass_shift * values + owned


def squares(residual):
    return lax.psum(jnp.sum(residual * residual), ("row", "col"))


def per_device(
    connectivity,
    gradients,
    volumes,
    live_blocks,
    send_lists,
    divergence,
    mass_shift,
    boundary_nodes,
    surface_points,
    normal_cos,
    normal_angle,
    node_areas,
):
    potential = jnp.zeros_like(divergence)
    residual = divergence
    direction = divergence
    norm_now = squares(residual)
    for iteration in range(ITERS):
        image = apply_operator(
            direction, connectivity, gradients, volumes, live_blocks, send_lists, mass_shift
        )
        alpha = norm_now / lax.psum(jnp.sum(direction * image), ("row", "col"))
        potential = potential + alpha * direction
        residual = residual - alpha * image
        norm_next = squares(residual)
        direction = residual + norm_next / norm_now * direction
        norm_now = norm_next
    traces = potential[boundary_nodes]
    trace_bf = traces.astype(jnp.bfloat16)
    sine = jnp.sqrt(1.0 - normal_cos * normal_cos)
    normals = jnp.stack([sine * jnp.cos(normal_angle), sine * jnp.sin(normal_angle), normal_cos])
    weighted = node_areas[None, :] * normals
    sources = jnp.concatenate(
        [surface_points, weighted, trace_bf.astype(jnp.float32)[None, :]], axis=0
    )
    target_points = surface_points[:, :TGT_DEV]
    target_traces = traces[:TGT_DEV]
    piece = lax.all_gather(sources, ("row", "col"), axis=1, tiled=True)
    width = piece.shape[1]
    step = pick_block(width, 4096)

    def add_part(part_index, running):
        columns = lax.dynamic_slice_in_dim(piece, part_index * step, step, 1)
        return running + kernel_rows(target_points, columns)

    far_field = lax.fori_loop(0, width // step, add_part, jnp.zeros((TGT_DEV,), jnp.float32))
    dirichlet = far_field - 0.5 * target_traces
    return (potential, dirichlet)


def solution(mesh):
    return jax.shard_map(
        per_device,
        mesh=mesh,
        in_specs=(
            P(None, ("row", "col")),
            P(None, ("row", "col")),
            P(("row", "col")),
            P(("row", "col")),
            P(None, ("row", "col")),
            P(("row", "col")),
            P(("row", "col")),
            P(("row", "col")),
            P(None, ("row", "col")),
            P(("row", "col")),
            P(("row", "col")),
            P(("row", "col")),
        ),
        out_specs=(P(("row", "col")), P(("row", "col"))),
        check_vma=False,
    )
```

profile of v0, /device:TPU:1, one launch (start us, length us, event | category | flops | bytes accessed | tf_op | source)
XLA Modules:
  0.0 1841.5 jit_solution(16345966479136023931)
XLA Ops:
  8.0 6.2 gather_fusion.3
  14.2 4.5 collective-permute-start
  18.7 1.9 collective-permute-start.1
  20.7 2.9 collective-permute-done.1
  23.6 3.5 collective-permute-start.2
  28.6 3.2 collective-permute-done.3
  31.8 144.6 %while.44 = (s32[]{:T(128)}, f32[3072]{0:T(1024)S(1)}, s32[]{:T(128)}, s32[4,8192]{1,0:T(4,128)S(1)}, f32[9,8192]{1,0:T(8,128)}, /*index=5*/f32[3072]{0:T(1024)S...) while((s32[]{:T(128)}, f32[3072]{0:T(1024)S(1)}, s32[]{:T(128)}, ...), condition=%wide.region_8.0_spmd, body=%wide.region_2.0_spmd.sunk | while | flops 88072 | bytes 393431 | solution.py:111
  32.5 23.0 %gather_fusion = f32[4096]{0:T(1024)S(1)} fusion(f32[3072]{0:T(1024)S(1)} %get-tuple-element.611, s32[4096]{0:T(1024)S(1)} %broadcast_clamp_fusion.7), kind=kCustom, calls=%fused_computation.clone.1 | custom fusion | bytes 49152 | tf_op jit(solution)/shard_map/while/body/gather | solution.py:35
  57.4 22.4 %scatter_fusion = f32[3072]{0:T(1024)S(1)} fusion(f32[3072]{0:T(1024)S(1)} %get-tuple-element.594, s32[4096]{0:T(1024)S(1)} %bitcast.295, f32[4096]{0:T(1024)S(1)} %bitcast.292), kind=kCustom, calls=%fused_computation.7.clone.1 | custom fusion | flops 4096 | bytes 65536 | tf_op jit(solution)/shard_map/while/body/scatter-add | solution.py:109
  80.4 23.0 %gather_fusion = f32[4096]{0:T(1024)S(1)} fusion(f32[3072]{0:T(1024)S(1)} %get-tuple-element.611, s32[4096]{0:T(1024)S(1)} %broadcast_clamp_fusion.7), kind=kCustom, calls=%fused_computation.clone.1 | custom fusion | bytes 49152 | tf_op jit(solution)/shard_map/while/body/gather | solution.py:35
  105.3 22.4 %scatter_fusion = f32[3072]{0:T(1024)S(1)} fusion(f32[3072]{0:T(1024)S(1)} %get-tuple-element.594, s32[4096]{0:T(1024)S(1)} %bitcast.295, f32[4096]{0:T(1024)S(1)} %bitcast.292), kind=kCustom, calls=%fused_computation.7.clone.1 | custom fusion | flops 4096 | bytes 65536 | tf_op jit(solution)/shard_map/while/body/scatter-add | solution.py:109
  128.4 23.0 %gather_fusion = f32[4096]{0:T(1024)S(1)} fusion(f32[3072]{0:T(1024)S(1)} %get-tuple-element.611, s32[4096]{0:T(1024)S(1)} %broadcast_clamp_fusion.7), kind=kCustom, calls=%fused_computation.clone.1 | custom fusion | bytes 49152 | tf_op jit(solution)/shard_map/while/body/gather | solution.py:35
  153.3 22.4 %scatter_fusion = f32[3072]{0:T(1024)S(1)} fusion(f32[3072]{0:T(1024)S(1)} %get-tuple-element.594, s32[4096]{0:T(1024)S(1)} %bitcast.295, f32[4096]{0:T(1024)S(1)} %bitcast.292), kind=kCustom, calls=%fused_computation.7.clone.1 | custom fusion | flops 4096 | bytes 65536 | tf_op jit(solution)/shard_map/while/body/scatter-add | solution.py:109
  176.4 1.9 collective-permute-start.5
  178.3 48.7 %collective-permute-start.4 = (f32[1,3,256]{2,1,0:T(4,128)S(1)}, f32[1,3,256]{2,1,0:T(4,128)S(1)}, u32[]{:S(2)}, u32[]{:S(2)}) collective-permute-start(f32[1,3,256]{2,1,0:T(4,128)S(1)} %get-tuple-element.353), channel_id=1, source_target_pairs={{32,0},{64,32},{96,64},{128,96},{160,128},{192,160},{224,192},{33,... | collective-permute-start | bytes 9224 | tf_op jit(solution)/shard_map/ppermute | solution.py:22
  230.5 58.1 %collective-permute-done.6 = f32[5,1,256]{2,1,0:T(1,128)S(1)} collective-permute-done((f32[5,1,256]{2,1,0:T(1,128)S(1)}, f32[5,1,256]{2,1,0:T(1,128)S(1)}, u32[]{:S(2)}, u32[]{:S(2)}) %collective-permute-start.6) | collective-permute-done | bytes 5152 | tf_op jit(solution)/shard_map/ppermute | solution.py:22
  288.6 6.1 scatter_fusion.3
  295.3 218.7 %all-reduce = (f32[]{:T(128)}, f32[]{:T(128)}) all-reduce(f32[]{:T(128)} %get-tuple-element.227, f32[]{:T(128)} %get-tuple-element.226), channel_id=1, replica_groups=mesh['row'=8,'col'=32] {'row','col'}, use_global_device_ids=true, to_apply=%region_1.0 | all-reduce | flops 2 | bytes 16 | tf_op jit(solution)/shard_map/psum | solution.py:119
  516.0 72.5 %psum.44 = f32[]{:T(128)} all-reduce(f32[]{:T(128)} %get-tuple-element.284), channel_id=1, replica_groups=mesh['row'=8,'col'=32] {'row','col'}, use_global_device_ids=true, to_apply=%region_13.0 | all-reduce | flops 1 | bytes 8 | tf_op jit(solution)/shard_map/psum | solution.py:119
  589.9 6.2 gather_fusion.4
  596.1 3.3 collective-permute-start.8
  599.5 1.9 collective-permute-start.9
  601.5 2.9 collective-permute-done.9
  604.4 3.7 collective-permute-start.10
  609.5 3.0 collective-permute-done.11
  612.5 144.6 %while.45 = (s32[]{:T(128)}, f32[3072]{0:T(1024)S(1)}, s32[]{:T(128)}, s32[4,8192]{1,0:T(4,128)S(1)}, f32[9,8192]{1,0:T(8,128)}, /*index=5*/f32[3072]{0:T(1024)S...) while((s32[]{:T(128)}, f32[3072]{0:T(1024)S(1)}, s32[]{:T(128)}, ...), condition=%wide.region_20.0_spmd, body=%wide.region_14.0_spmd.sunk | while | flops 88072 | bytes 393431 | solution.py:111
  613.2 23.0 %gather_fusion.1 = f32[4096]{0:T(1024)S(1)} fusion(f32[3072]{0:T(1024)S(1)} %get-tuple-element.650, s32[4096]{0:T(1024)S(1)} %broadcast_clamp_fusion.8), kind=kCustom, calls=%fused_computation.1.clone.1 | custom fusion | bytes 49152 | tf_op jit(solution)/shard_map/while/body/gather | solution.py:35
  638.1 22.4 %scatter_fusion.1 = f32[3072]{0:T(1024)S(1)} fusion(f32[3072]{0:T(1024)S(1)} %get-tuple-element.633, s32[4096]{0:T(1024)S(1)} %bitcast.296, f32[4096]{0:T(1024)S(1)} %bitcast.293), kind=kCustom, calls=%fused_computation.8.clone.1 | custom fusion | flops 4096 | bytes 65536 | tf_op jit(solution)/shard_map/while/body/scatter-add | solution.py:109
  661.1 23.0 %gather_fusion.1 = f32[4096]{0:T(1024)S(1)} fusion(f32[3072]{0:T(1024)S(1)} %get-tuple-element.650, s32[4096]{0:T(1024)S(1)} %broadcast_clamp_fusion.8), kind=kCustom, calls=%fused_computation.1.clone.1 | custom fusion | bytes 49152 | tf_op jit(solution)/shard_map/while/body/gather | solution.py:35
  686.0 22.4 %scatter_fusion.1 = f32[3072]{0:T(1024)S(1)} fusion(f32[3072]{0:T(1024)S(1)} %get-tuple-element.633, s32[4096]{0:T(1024)S(1)} %bitcast.296, f32[4096]{0:T(1024)S(1)} %bitcast.293), kind=kCustom, calls=%fused_computation.8.clone.1 | custom fusion | flops 4096 | bytes 65536 | tf_op jit(solution)/shard_map/while/body/scatter-add | solution.py:109
  709.1 23.0 %gather_fusion.1 = f32[4096]{0:T(1024)S(1)} fusion(f32[3072]{0:T(1024)S(1)} %get-tuple-element.650, s32[4096]{0:T(1024)S(1)} %broadcast_clamp_fusion.8), kind=kCustom, calls=%fused_computation.1.clone.1 | custom fusion | bytes 49152 | tf_op jit(solution)/shard_map/while/body/gather | solution.py:35
  734.0 22.4 %scatter_fusion.1 = f32[3072]{0:T(1024)S(1)} fusion(f32[3072]{0:T(1024)S(1)} %get-tuple-element.633, s32[4096]{0:T(1024)S(1)} %bitcast.296, f32[4096]{0:T(1024)S(1)} %bitcast.293), kind=kCustom, calls=%fused_computation.8.clone.1 | custom fusion | flops 4096 | bytes 65536 | tf_op jit(solution)/shard_map/while/body/scatter-add | solution.py:109
  757.1 1.9 collective-permute-start.13
  759.0 48.9 %collective-permute-start.12 = (f32[1,3,256]{2,1,0:T(4,128)S(1)}, f32[1,3,256]{2,1,0:T(4,128)S(1)}, u32[]{:S(2)}, u32[]{:S(2)}) collective-permute-start(f32[1,3,256]{2,1,0:T(4,128)S(1)} %get-tuple-element.349), channel_id=1, source_target_pairs={{32,0},{64,32},{96,64},{128,96},{160,128},{192,160},{224,192},{33,... | collective-permute-start | bytes 9224 | tf_op jit(solution)/shard_map/ppermute | solution.py:22
  811.4 53.7 %collective-permute-done.14 = f32[5,1,256]{2,1,0:T(1,128)S(1)} collective-permute-done((f32[5,1,256]{2,1,0:T(1,128)S(1)}, f32[5,1,256]{2,1,0:T(1,128)S(1)}, u32[]{:S(2)}, u32[]{:S(2)}) %collective-permute-start.14) | collective-permute-done | bytes 5152 | tf_op jit(solution)/shard_map/ppermute | solution.py:22
  865.1 6.1 scatter_fusion.4
  871.8 216.6 %psum.45 = f32[]{:T(128)} all-reduce(f32[]{:T(128)} %multiply_reduce_fusion.14), channel_id=1, replica_groups=mesh['row'=8,'col'=32] {'row','col'}, use_global_device_ids=true, to_apply=%region_23.0 | all-reduce | flops 1 | bytes 8 | tf_op jit(solution)/shard_map/psum | solution.py:144
  1090.4 73.1 %psum.46 = f32[]{:T(128)} all-reduce(f32[]{:T(128)} %multiply_reduce_fusion.13), channel_id=1, replica_groups=mesh['row'=8,'col'=32] {'row','col'}, use_global_device_ids=true, to_apply=%region_25.0 | all-reduce | flops 1 | bytes 8 | tf_op jit(solution)/shard_map/psum | solution.py:119
  1164.8 6.2 gather_fusion.5
  1171.0 3.0 collective-permute-start.16
  1174.0 1.9 collective-permute-start.17
  1176.0 2.9 collective-permute-done.17
  1179.0 3.7 collective-permute-start.18
  1184.0 3.0 collective-permute-done.19
  1187.0 144.6 %while.46 = (s32[]{:T(128)}, f32[3072]{0:T(1024)S(1)}, s32[]{:T(128)}, s32[4,8192]{1,0:T(4,128)S(1)}, f32[9,8192]{1,0:T(8,128)}, /*index=5*/f32[3072]{0:T(1024)S...) while((s32[]{:T(128)}, f32[3072]{0:T(1024)S(1)}, s32[]{:T(128)}, ...), condition=%wide.region_32.0_spmd, body=%wide.region_26.0_spmd.sunk | while | flops 88072 | bytes 393431 | solution.py:111
  1187.7 23.0 %gather_fusion.2 = f32[4096]{0:T(1024)S(1)} fusion(f32[3072]{0:T(1024)S(1)} %get-tuple-element.689, s32[4096]{0:T(1024)S(1)} %broadcast_clamp_fusion.9), kind=kCustom, calls=%fused_computation.2.clone.1 | custom fusion | bytes 49152 | tf_op jit(solution)/shard_map/while/body/gather | solution.py:35
  1212.6 22.4 %scatter_fusion.2 = f32[3072]{0:T(1024)S(1)} fusion(f32[3072]{0:T(1024)S(1)} %get-tuple-element.672, s32[4096]{0:T(1024)S(1)} %bitcast.297, f32[4096]{0:T(1024)S(1)} %bitcast.294), kind=kCustom, calls=%fused_computation.9.clone.1 | custom fusion | flops 4096 | bytes 65536 | tf_op jit(solution)/shard_map/while/body/scatter-add | solution.py:109
  1235.7 23.0 %gather_fusion.2 = f32[4096]{0:T(1024)S(1)} fusion(f32[3072]{0:T(1024)S(1)} %get-tuple-element.689, s32[4096]{0:T(1024)S(1)} %broadcast_clamp_fusion.9), kind=kCustom, calls=%fused_computation.2.clone.1 | custom fusion | bytes 49152 | tf_op jit(solution)/shard_map/while/body/gather | solution.py:35
  1260.6 22.4 %scatter_fusion.2 = f32[3072]{0:T(1024)S(1)} fusion(f32[3072]{0:T(1024)S(1)} %get-tuple-element.672, s32[4096]{0:T(1024)S(1)} %bitcast.297, f32[4096]{0:T(1024)S(1)} %bitcast.294), kind=kCustom, calls=%fused_computation.9.clone.1 | custom fusion | flops 4096 | bytes 65536 | tf_op jit(solution)/shard_map/while/body/scatter-add | solution.py:109
  1283.7 23.0 %gather_fusion.2 = f32[4096]{0:T(1024)S(1)} fusion(f32[3072]{0:T(1024)S(1)} %get-tuple-element.689, s32[4096]{0:T(1024)S(1)} %broadcast_clamp_fusion.9), kind=kCustom, calls=%fused_computation.2.clone.1 | custom fusion | bytes 49152 | tf_op jit(solution)/shard_map/while/body/gather | solution.py:35
  1308.6 22.4 %scatter_fusion.2 = f32[3072]{0:T(1024)S(1)} fusion(f32[3072]{0:T(1024)S(1)} %get-tuple-element.672, s32[4096]{0:T(1024)S(1)} %bitcast.297, f32[4096]{0:T(1024)S(1)} %bitcast.294), kind=kCustom, calls=%fused_computation.9.clone.1 | custom fusion | flops 4096 | bytes 65536 | tf_op jit(solution)/shard_map/while/body/scatter-add | solution.py:109
  1331.6 1.9 collective-permute-start.21
  1333.6 48.9 %collective-permute-start.20 = (f32[1,3,256]{2,1,0:T(4,128)S(1)}, f32[1,3,256]{2,1,0:T(4,128)S(1)}, u32[]{:S(2)}, u32[]{:S(2)}) collective-permute-start(f32[1,3,256]{2,1,0:T(4,128)S(1)} %get-tuple-element.345), channel_id=1, source_target_pairs={{32,0},{64,32},{96,64},{128,96},{160,128},{192,160},{224,192},{33,... | collective-permute-start | bytes 9224 | tf_op jit(solution)/shard_map/ppermute | solution.py:22
  1385.9 53.7 %collective-permute-done.22 = f32[5,1,256]{2,1,0:T(1,128)S(1)} collective-permute-done((f32[5,1,256]{2,1,0:T(1,128)S(1)}, f32[5,1,256]{2,1,0:T(1,128)S(1)}, u32[]{:S(2)}, u32[]{:S(2)}) %collective-permute-start.22) | collective-permute-done | bytes 5152 | tf_op jit(solution)/shard_map/ppermute | solution.py:22
  1439.6 6.1 scatter_fusion.5
  1446.4 216.6 %psum.47 = f32[]{:T(128)} all-reduce(f32[]{:T(128)} %multiply_reduce_fusion.12), channel_id=1, replica_groups=mesh['row'=8,'col'=32] {'row','col'}, use_global_device_ids=true, to_apply=%region_35.0 | all-reduce | flops 1 | bytes 8 | tf_op jit(solution)/shard_map/psum | solution.py:144
  1664.3 2.2 gather_fusion.6
  1667.3 100.3 %all-gather.3.cloned.1.call-done = f32[256,320,7]{1,2,0:T(8,128)} async-done(((f32[1,320,7]{1,2,0:T(8,128)}), f32[256,320,7]{1,2,0:T(8,128)}) %all-gather.3.cloned.1.call-update) | async-done | bytes 2293776 | tf_op jit(solution)/shard_map/all_gather | solution.py:160
  1767.5 2.4 copy.16
  1770.0 2.8 reshape.207
  1772.8 61.3 %while.47 = (s32[]{:T(128)}, f32[32]{0:T(128)S(1)}, f32[3,32]{1,0:T(4,128)S(1)}, f32[7,81920]{1,0:T(8,128)}, s32[]{:T(128)}, /*index=5*/s32[]{:T(128)}, s32[]{:T...) while((s32[]{:T(128)}, f32[32]{0:T(128)S(1)}, f32[3,32]{1,0:T(4,128)S(1)}, ...), condition=%wide.region_37.0_spmd.clone, body=%wide.region_36.0_spmd.clone.sunk | while | flops 2752589 | bytes 312997 | solution.py:168
  1782.0 1.8 constant_dynamic-slice_fusion.2
  1794.4 1.8 constant_dynamic-slice_fusion.2
  1818.9 1.8 constant_dynamic-slice_fusion.2
  (296 shorter events, 91.9 us)
Async XLA Ops:
  7.2 0.8 copy-start
  7.2 24.6 %copy-start.2 = (s32[4,8192]{1,0:T(4,128)S(1)}, s32[4,8192]{1,0:T(4,128)}, u32[]{:S(2)}) copy-start(s32[4,8192]{1,0:T(4,128)} %param.20) | copy-start | bytes 393220
  7.2 1760.3 %all-gather.3.cloned.1.call-start = ((), (), s32[]{:S(2)}) async-start(), calls=%async_computation | async-start | bytes 3158016 | tf_op jit(solution)/shard_map/all_gather | solution.py:160
  14.2 6.4 collective-permute-start
  18.7 4.9 collective-permute-start.1
  23.6 4.9 collective-permute-start.2
  27.2 4.6 collective-permute-start.3
  31.7 195.3 %copy-start.3 = (f32[2048]{0:T(1024)S(1)}, f32[2048]{0:T(1024)}, u32[]{:S(2)}) copy-start(f32[2048]{0:T(1024)} %param.26) | copy-start | bytes 24580
  176.4 50.6 %collective-permute-start.5 = (f32[1,3,256]{2,1,0:T(4,128)S(1)}, f32[1,3,256]{2,1,0:T(4,128)S(1)}, u32[]{:S(2)}, u32[]{:S(2)}) collective-permute-start(f32[1,3,256]{2,1,0:T(4,128)S(1)} %get-tuple-element.354), channel_id=1, source_target_pairs={{0,32},{32,64},{64,96},{96,128},{128,160},{160,192},{192,224},{1,3... | collective-permute-start | bytes 9224 | tf_op jit(solution)/shard_map/ppermute | solution.py:19
  178.3 49.5 %collective-permute-start.4 = (f32[1,3,256]{2,1,0:T(4,128)S(1)}, f32[1,3,256]{2,1,0:T(4,128)S(1)}, u32[]{:S(2)}, u32[]{:S(2)}) collective-permute-start(f32[1,3,256]{2,1,0:T(4,128)S(1)} %get-tuple-element.353), channel_id=1, source_target_pairs={{32,0},{64,32},{96,64},{128,96},{160,128},{192,160},{224,192},{33,... | collective-permute-start | bytes 9224 | tf_op jit(solution)/shard_map/ppermute | solution.py:22
  227.8 2.6 collective-permute-start.7
  229.1 59.4 %collective-permute-start.6 = (f32[5,1,256]{2,1,0:T(1,128)S(1)}, f32[5,1,256]{2,1,0:T(1,128)S(1)}, u32[]{:S(2)}, u32[]{:S(2)}) collective-permute-start(f32[5,1,256]{2,1,0:T(1,128)S(1)} %get-tuple-element.315), channel_id=1, source_target_pairs={{1,0},{2,1},{3,2},{4,3},{5,4},{6,5},{7,6},{8,7},{9,8},{10,9},{11,1... | collective-permute-start | bytes 15368 | tf_op jit(solution)/shard_map/ppermute | solution.py:22
  294.7 304.7 %copy-start.5 = (f32[320]{0:T(512)S(1)}, f32[320]{0:T(512)}, u32[]{:S(2)}) copy-start(f32[320]{0:T(512)} %param.29) | copy-start | bytes 3844
  294.7 304.7 %copy-start.8 = (f32[320]{0:T(512)S(1)}, f32[320]{0:T(512)}, u32[]{:S(2)}) copy-start(f32[320]{0:T(512)} %param.30) | copy-start | bytes 3844
  596.1 5.3 collective-permute-start.8
  599.5 4.9 collective-permute-start.9
  604.4 5.0 collective-permute-start.10
  608.1 4.4 collective-permute-start.11
  757.1 50.8 %collective-permute-start.13 = (f32[1,3,256]{2,1,0:T(4,128)S(1)}, f32[1,3,256]{2,1,0:T(4,128)S(1)}, u32[]{:S(2)}, u32[]{:S(2)}) collective-permute-start(f32[1,3,256]{2,1,0:T(4,128)S(1)} %get-tuple-element.350), channel_id=1, source_target_pairs={{0,32},{32,64},{64,96},{96,128},{128,160},{160,192},{192,224},{1,3... | collective-permute-start | bytes 9224 | tf_op jit(solution)/shard_map/ppermute | solution.py:19
  759.0 49.7 %collective-permute-start.12 = (f32[1,3,256]{2,1,0:T(4,128)S(1)}, f32[1,3,256]{2,1,0:T(4,128)S(1)}, u32[]{:S(2)}, u32[]{:S(2)}) collective-permute-start(f32[1,3,256]{2,1,0:T(4,128)S(1)} %get-tuple-element.349), channel_id=1, source_target_pairs={{32,0},{64,32},{96,64},{128,96},{160,128},{192,160},{224,192},{33,... | collective-permute-start | bytes 9224 | tf_op jit(solution)/shard_map/ppermute | solution.py:22
  808.7 2.6 collective-permute-start.15
  810.0 55.0 %collective-permute-start.14 = (f32[5,1,256]{2,1,0:T(1,128)S(1)}, f32[5,1,256]{2,1,0:T(1,128)S(1)}, u32[]{:S(2)}, u32[]{:S(2)}) collective-permute-start(f32[5,1,256]{2,1,0:T(1,128)S(1)} %get-tuple-element.311), channel_id=1, source_target_pairs={{1,0},{2,1},{3,2},{4,3},{5,4},{6,5},{7,6},{8,7},{9,8},{10,9},{11,1... | collective-permute-start | bytes 15368 | tf_op jit(solution)/shard_map/ppermute | solution.py:22
  865.1 225.3 %copy-start.6 = (f32[320]{0:T(512)S(1)}, f32[320]{0:T(512)}, u32[]{:S(2)}) copy-start(f32[320]{0:T(512)} %param.31) | copy-start | bytes 3844
  871.2 302.8 %copy-start.7 = (s32[320]{0:T(512)S(1)}, s32[320]{0:T(512)}, u32[]{:S(2)}) copy-start(s32[320]{0:T(512)} %param.27) | copy-start | bytes 3844
  1171.0 5.0 collective-permute-start.16
  1174.0 4.9 collective-permute-start.17
  1179.0 5.0 collective-permute-start.18
  1182.6 4.4 collective-permute-start.19
  1331.6 50.8 %collective-permute-start.21 = (f32[1,3,256]{2,1,0:T(4,128)S(1)}, f32[1,3,256]{2,1,0:T(4,128)S(1)}, u32[]{:S(2)}, u32[]{:S(2)}) collective-permute-start(f32[1,3,256]{2,1,0:T(4,128)S(1)} %get-tuple-element.346), channel_id=1, source_target_pairs={{0,32},{32,64},{64,96},{96,128},{128,160},{160,192},{192,224},{1,3... | collective-permute-start | bytes 9224 | tf_op jit(solution)/shard_map/ppermute | solution.py:19
  1333.6 49.7 %collective-permute-start.20 = (f32[1,3,256]{2,1,0:T(4,128)S(1)}, f32[1,3,256]{2,1,0:T(4,128)S(1)}, u32[]{:S(2)}, u32[]{:S(2)}) collective-permute-start(f32[1,3,256]{2,1,0:T(4,128)S(1)} %get-tuple-element.345), channel_id=1, source_target_pairs={{32,0},{64,32},{96,64},{128,96},{160,128},{192,160},{224,192},{33,... | collective-permute-start | bytes 9224 | tf_op jit(solution)/shard_map/ppermute | solution.py:22
  1383.3 2.6 collective-permute-start.23
  1384.6 55.0 %collective-permute-start.22 = (f32[5,1,256]{2,1,0:T(1,128)S(1)}, f32[5,1,256]{2,1,0:T(1,128)S(1)}, u32[]{:S(2)}, u32[]{:S(2)}) collective-permute-start(f32[5,1,256]{2,1,0:T(1,128)S(1)} %get-tuple-element.307), channel_id=1, source_target_pairs={{1,0},{2,1},{3,2},{4,3},{5,4},{6,5},{7,6},{8,7},{9,8},{10,9},{11,1... | collective-permute-start | bytes 15368 | tf_op jit(solution)/shard_map/ppermute | solution.py:22
  1439.6 227.0 %copy-start.4 = (f32[3,320]{1,0:T(4,128)S(1)}, f32[3,320]{1,0:T(4,128)}, u32[]{:S(2)}) copy-start(f32[3,320]{1,0:T(4,128)} %param.28) | copy-start | bytes 11524
  1664.3 105.6 %copy-start.1 = (f32[2048]{0:T(1024)}, f32[2048]{0:T(1024)S(1)}, u32[]{:S(2)}) copy-start(f32[2048]{0:T(1024)S(1)} %multiply_add_fusion.3) | copy-start | bytes 24580
  1770.0 2.9 slice-start
Sparse Core Ops, SparseCore 0:
  1667.4 100.1 all-gather.2
where the time goes:
time: 1850 us; the launch traced here: 1840 us
  blocking collectives  798 us (43%)
  waiting for transfers between devices  286 us (15%)
  local copies, waits for them, and re-layouts  272 us (15%)
  other arithmetic  235 us (13%)
  starting transfers between devices  191 us (10%)
  matrix products  28.8 us (2%)
  between operations  21.8 us (1%)
    psum x2, blocking collectives, per_device(): alpha = norm_now / lax.psum(jnp.sum(direction * image), ('row', 'col'))  433 us
    psum x3, blocking collectives, squares(): return lax.psum(jnp.sum(residual * residual), ('row', 'col'))  364 us
    gather x9, local copies, waits for them, and re-layouts, element_terms(): corner_values = extended[corners]  207 us
    scatter-add x9, other arithmetic, add_block(): total.at[corners]  201 us
    ppermute x12, waiting for transfers between devices, with_halo(): lax.ppermute(lax.slice_in_dim(block, 0, width, axis=dim), axis, backward)  185 us
    ppermute x12, starting transfers between devices, with_halo(): lax.ppermute(lax.slice_in_dim(block, 0, width, axis=dim), axis, backward)  160 us
    all_gather x1, waiting for transfers between devices, per_device(): piece = lax.all_gather(sources, ('row', 'col'), axis=1, tiled=True)  100 us
  transfers between devices with their start and end apart: 25, of which 13 were waited for; matrix products, arithmetic and copies ran while one was open for 0% of the time, Pallas kernels for 0%

commit v1 on v0

--- a/solution.py
+++ b/solution.py
@@ -157,7 +157,8 @@
     )
     target_points = surface_points[:, :TGT_DEV]
     target_traces = traces[:TGT_DEV]
-    piece = lax.all_gather(sources, ("row", "col"), axis=1, tiled=True)
+    outgoing = jnp.stack([sources] * lax.axis_size(("row", "col")))
+    piece = jnp.concatenate(lax.all_to_all(outgoing, ("row", "col"), 0, 0), axis=1)
     width = piece.shape[1]
     step = pick_block(width, 4096)
 

time: 1850 us -> 1770 us (0.957)
  local copies, waits for them, and re-layouts: 272 us -> 247 us
  waiting for transfers between devices: 286 us -> 262 us
    all_gather x1 -> x0, waiting for transfers between devices: 100 us -> none  [per_device(): piece = lax.all_gather(sources, ('row', 'col'), axis=1, tiled=True)]
    all_to_all x0 -> x1, waiting for transfers between devices: none -> 76.4 us  [per_device(): lax.all_to_all(outgoing, ('row', 'col'), 0, 0)]
    slice x20, local copies, waits for them, and re-layouts: 32.1 us -> 4.99 us  [kernel_rows(): delta_x = targets[0][:, None] - sources[0][None, :]]
where the time goes in v1:
time: 1770 us
  blocking collectives  798 us (45%)
  waiting for transfers between devices  262 us (15%)
  local copies, waits for them, and re-layouts  247 us (14%)
  other arithmetic  235 us (13%)
  starting transfers between devices  198 us (11%)
    psum x2, blocking collectives, per_device(): alpha = norm_now / lax.psum(jnp.sum(direction * image), ('row', 'col'))  433 us
    psum x3, blocking collectives, squares(): return lax.psum(jnp.sum(residual * residual), ('row', 'col'))  364 us
    gather x9, local copies, waits for them, and re-layouts, element_terms(): corner_values = extended[corners]  207 us
    scatter-add x9, other arithmetic, add_block(): total.at[corners]  201 us
    ppermute x12, waiting for transfers between devices, with_halo(): lax.ppermute(lax.slice_in_dim(block, 0, width, axis=dim), axis, backward)  185 us
    ppermute x12, starting transfers between devices, with_halo(): lax.ppermute(lax.slice_in_dim(block, 0, width, axis=dim), axis, backward)  160 us
    all_to_all x1, waiting for transfers between devices, per_device(): lax.all_to_all(outgoing, ('row', 'col'), 0, 0)  76.4 us
  transfers between devices with their start and end apart: 25, of which 13 were waited for; matrix products, arithmetic and copies ran while one was open for 0% of the time, Pallas kernels for 0%

profile of v1, /device:TPU:1, one launch (start us, length us, event | category | flops | bytes accessed | tf_op | source)
XLA Modules:
  0.0 1766.7 jit_solution(1143407738781331305)
XLA Ops:
  1.4 6.2 gather_fusion.3
  7.6 4.5 collective-permute-start
  12.1 1.9 collective-permute-start.1
  14.1 2.9 collective-permute-done.1
  17.1 3.5 collective-permute-start.2
  22.0 3.2 collective-permute-done.3
  25.2 144.6 %while.44 = (s32[]{:T(128)}, f32[3072]{0:T(1024)S(1)}, s32[]{:T(128)}, s32[4,8192]{1,0:T(4,128)S(1)}, f32[9,8192]{1,0:T(8,128)}, /*index=5*/f32[3072]{0:T(1024)S...) while((s32[]{:T(128)}, f32[3072]{0:T(1024)S(1)}, s32[]{:T(128)}, ...), condition=%wide.region_8.0_spmd, body=%wide.region_2.0_spmd.sunk | while | flops 88072 | bytes 393431 | solution.py:111
  25.9 23.0 %gather_fusion = f32[4096]{0:T(1024)S(1)} fusion(f32[3072]{0:T(1024)S(1)} %get-tuple-element.611, s32[4096]{0:T(1024)S(1)} %broadcast_clamp_fusion.7), kind=kCustom, calls=%fused_computation.clone.1 | custom fusion | bytes 49152 | tf_op jit(solution)/shard_map/while/body/gather | solution.py:35
  50.8 22.4 %scatter_fusion = f32[3072]{0:T(1024)S(1)} fusion(f32[3072]{0:T(1024)S(1)} %get-tuple-element.594, s32[4096]{0:T(1024)S(1)} %bitcast.289, f32[4096]{0:T(1024)S(1)} %bitcast.286), kind=kCustom, calls=%fused_computation.7.clone.1 | custom fusion | flops 4096 | bytes 65536 | tf_op jit(solution)/shard_map/while/body/scatter-add | solution.py:109
  73.9 23.0 %gather_fusion = f32[4096]{0:T(1024)S(1)} fusion(f32[3072]{0:T(1024)S(1)} %get-tuple-element.611, s32[4096]{0:T(1024)S(1)} %broadcast_clamp_fusion.7), kind=kCustom, calls=%fused_computation.clone.1 | custom fusion | bytes 49152 | tf_op jit(solution)/shard_map/while/body/gather | solution.py:35
  98.8 22.4 %scatter_fusion = f32[3072]{0:T(1024)S(1)} fusion(f32[3072]{0:T(1024)S(1)} %get-tuple-element.594, s32[4096]{0:T(1024)S(1)} %bitcast.289, f32[4096]{0:T(1024)S(1)} %bitcast.286), kind=kCustom, calls=%fused_computation.7.clone.1 | custom fusion | flops 4096 | bytes 65536 | tf_op jit(solution)/shard_map/while/body/scatter-add | solution.py:109
  121.8 23.0 %gather_fusion = f32[4096]{0:T(1024)S(1)} fusion(f32[3072]{0:T(1024)S(1)} %get-tuple-element.611, s32[4096]{0:T(1024)S(1)} %broadcast_clamp_fusion.7), kind=kCustom, calls=%fused_computation.clone.1 | custom fusion | bytes 49152 | tf_op jit(solution)/shard_map/while/body/gather | solution.py:35
  146.7 22.4 %scatter_fusion = f32[3072]{0:T(1024)S(1)} fusion(f32[3072]{0:T(1024)S(1)} %get-tuple-element.594, s32[4096]{0:T(1024)S(1)} %bitcast.289, f32[4096]{0:T(1024)S(1)} %bitcast.286), kind=kCustom, calls=%fused_computation.7.clone.1 | custom fusion | flops 4096 | bytes 65536 | tf_op jit(solution)/shard_map/while/body/scatter-add | solution.py:109
  169.8 1.9 collective-permute-start.5
  171.7 48.7 %collective-permute-start.4 = (f32[1,3,256]{2,1,0:T(4,128)S(1)}, f32[1,3,256]{2,1,0:T(4,128)S(1)}, u32[]{:S(2)}, u32[]{:S(2)}) collective-permute-start(f32[1,3,256]{2,1,0:T(4,128)S(1)} %get-tuple-element.353), channel_id=1, source_target_pairs={{32,0},{64,32},{96,64},{128,96},{160,128},{192,160},{224,192},{33,... | collective-permute-start | bytes 9224 | tf_op jit(solution)/shard_map/ppermute | solution.py:22
  222.5 1.3 collective-permute-start.6
  223.9 58.1 %collective-permute-done.6 = f32[5,1,256]{2,1,0:T(1,128)S(1)} collective-permute-done((f32[5,1,256]{2,1,0:T(1,128)S(1)}, f32[5,1,256]{2,1,0:T(1,128)S(1)}, u32[]{:S(2)}, u32[]{:S(2)}) %collective-permute-start.6) | collective-permute-done | bytes 5152 | tf_op jit(solution)/shard_map/ppermute | solution.py:22
  282.0 6.1 scatter_fusion.3
  288.7 218.7 %all-reduce = (f32[]{:T(128)}, f32[]{:T(128)}) all-reduce(f32[]{:T(128)} %get-tuple-element.227, f32[]{:T(128)} %get-tuple-element.226), channel_id=1, replica_groups=mesh['row'=8,'col'=32] {'row','col'}, use_global_device_ids=true, to_apply=%region_1.0 | all-reduce | flops 2 | bytes 16 | tf_op jit(solution)/shard_map/psum | solution.py:119
  509.4 72.5 %psum.44 = f32[]{:T(128)} all-reduce(f32[]{:T(128)} %get-tuple-element.284), channel_id=1, replica_groups=mesh['row'=8,'col'=32] {'row','col'}, use_global_device_ids=true, to_apply=%region_13.0 | all-reduce | flops 1 | bytes 8 | tf_op jit(solution)/shard_map/psum | solution.py:119
  583.3 6.2 gather_fusion.4
  589.5 3.3 collective-permute-start.8
  592.9 1.9 collective-permute-start.9
  594.9 2.9 collective-permute-done.9
  597.8 3.7 collective-permute-start.10
  602.9 3.0 collective-permute-done.11
  605.9 144.6 %while.45 = (s32[]{:T(128)}, f32[3072]{0:T(1024)S(1)}, s32[]{:T(128)}, s32[4,8192]{1,0:T(4,128)S(1)}, f32[9,8192]{1,0:T(8,128)}, /*index=5*/f32[3072]{0:T(1024)S...) while((s32[]{:T(128)}, f32[3072]{0:T(1024)S(1)}, s32[]{:T(128)}, ...), condition=%wide.region_20.0_spmd, body=%wide.region_14.0_spmd.sunk | while | flops 88072 | bytes 393431 | solution.py:111
  606.6 23.0 %gather_fusion.1 = f32[4096]{0:T(1024)S(1)} fusion(f32[3072]{0:T(1024)S(1)} %get-tuple-element.650, s32[4096]{0:T(1024)S(1)} %broadcast_clamp_fusion.8), kind=kCustom, calls=%fused_computation.1.clone.1 | custom fusion | bytes 49152 | tf_op jit(solution)/shard_map/while/body/gather | solution.py:35
  631.5 22.4 %scatter_fusion.1 = f32[3072]{0:T(1024)S(1)} fusion(f32[3072]{0:T(1024)S(1)} %get-tuple-element.633, s32[4096]{0:T(1024)S(1)} %bitcast.290, f32[4096]{0:T(1024)S(1)} %bitcast.287), kind=kCustom, calls=%fused_computation.8.clone.1 | custom fusion | flops 4096 | bytes 65536 | tf_op jit(solution)/shard_map/while/body/scatter-add | solution.py:109
  654.6 23.0 %gather_fusion.1 = f32[4096]{0:T(1024)S(1)} fusion(f32[3072]{0:T(1024)S(1)} %get-tuple-element.650, s32[4096]{0:T(1024)S(1)} %broadcast_clamp_fusion.8), kind=kCustom, calls=%fused_computation.1.clone.1 | custom fusion | bytes 49152 | tf_op jit(solution)/shard_map/while/body/gather | solution.py:35
  679.5 22.4 %scatter_fusion.1 = f32[3072]{0:T(1024)S(1)} fusion(f32[3072]{0:T(1024)S(1)} %get-tuple-element.633, s32[4096]{0:T(1024)S(1)} %bitcast.290, f32[4096]{0:T(1024)S(1)} %bitcast.287), kind=kCustom, calls=%fused_computation.8.clone.1 | custom fusion | flops 4096 | bytes 65536 | tf_op jit(solution)/shard_map/while/body/scatter-add | solution.py:109
  702.5 23.0 %gather_fusion.1 = f32[4096]{0:T(1024)S(1)} fusion(f32[3072]{0:T(1024)S(1)} %get-tuple-element.650, s32[4096]{0:T(1024)S(1)} %broadcast_clamp_fusion.8), kind=kCustom, calls=%fused_computation.1.clone.1 | custom fusion | bytes 49152 | tf_op jit(solution)/shard_map/while/body/gather | solution.py:35
  727.4 22.4 %scatter_fusion.1 = f32[3072]{0:T(1024)S(1)} fusion(f32[3072]{0:T(1024)S(1)} %get-tuple-element.633, s32[4096]{0:T(1024)S(1)} %bitcast.290, f32[4096]{0:T(1024)S(1)} %bitcast.287), kind=kCustom, calls=%fused_computation.8.clone.1 | custom fusion | flops 4096 | bytes 65536 | tf_op jit(solution)/shard_map/while/body/scatter-add | solution.py:109
  750.5 1.9 collective-permute-start.13
  752.4 48.9 %collective-permute-start.12 = (f32[1,3,256]{2,1,0:T(4,128)S(1)}, f32[1,3,256]{2,1,0:T(4,128)S(1)}, u32[]{:S(2)}, u32[]{:S(2)}) collective-permute-start(f32[1,3,256]{2,1,0:T(4,128)S(1)} %get-tuple-element.349), channel_id=1, source_target_pairs={{32,0},{64,32},{96,64},{128,96},{160,128},{192,160},{224,192},{33,... | collective-permute-start | bytes 9224 | tf_op jit(solution)/shard_map/ppermute | solution.py:22
  804.8 53.7 %collective-permute-done.14 = f32[5,1,256]{2,1,0:T(1,128)S(1)} collective-permute-done((f32[5,1,256]{2,1,0:T(1,128)S(1)}, f32[5,1,256]{2,1,0:T(1,128)S(1)}, u32[]{:S(2)}, u32[]{:S(2)}) %collective-permute-start.14) | collective-permute-done | bytes 5152 | tf_op jit(solution)/shard_map/ppermute | solution.py:22
  858.5 6.1 scatter_fusion.4
  865.2 216.6 %psum.45 = f32[]{:T(128)} all-reduce(f32[]{:T(128)} %multiply_reduce_fusion.14), channel_id=1, replica_groups=mesh['row'=8,'col'=32] {'row','col'}, use_global_device_ids=true, to_apply=%region_23.0 | all-reduce | flops 1 | bytes 8 | tf_op jit(solution)/shard_map/psum | solution.py:144
  1083.8 73.1 %psum.46 = f32[]{:T(128)} all-reduce(f32[]{:T(128)} %multiply_reduce_fusion.13), channel_id=1, replica_groups=mesh['row'=8,'col'=32] {'row','col'}, use_global_device_ids=true, to_apply=%region_25.0 | all-reduce | flops 1 | bytes 8 | tf_op jit(solution)/shard_map/psum | solution.py:119
  1158.2 6.2 gather_fusion.5
  1164.4 3.0 collective-permute-start.16
  1167.4 1.9 collective-permute-start.17
  1169.4 2.9 collective-permute-done.17
  1172.4 3.7 collective-permute-start.18
  1177.5 3.0 collective-permute-done.19
  1180.5 144.6 %while.46 = (s32[]{:T(128)}, f32[3072]{0:T(1024)S(1)}, s32[]{:T(128)}, s32[4,8192]{1,0:T(4,128)S(1)}, f32[9,8192]{1,0:T(8,128)}, /*index=5*/f32[3072]{0:T(1024)S...) while((s32[]{:T(128)}, f32[3072]{0:T(1024)S(1)}, s32[]{:T(128)}, ...), condition=%wide.region_32.0_spmd, body=%wide.region_26.0_spmd.sunk | while | flops 88072 | bytes 393431 | solution.py:111
  1181.2 23.0 %gather_fusion.2 = f32[4096]{0:T(1024)S(1)} fusion(f32[3072]{0:T(1024)S(1)} %get-tuple-element.689, s32[4096]{0:T(1024)S(1)} %broadcast_clamp_fusion.9), kind=kCustom, calls=%fused_computation.2.clone.1 | custom fusion | bytes 49152 | tf_op jit(solution)/shard_map/while/body/gather | solution.py:35
  1206.1 22.4 %scatter_fusion.2 = f32[3072]{0:T(1024)S(1)} fusion(f32[3072]{0:T(1024)S(1)} %get-tuple-element.672, s32[4096]{0:T(1024)S(1)} %bitcast.291, f32[4096]{0:T(1024)S(1)} %bitcast.288), kind=kCustom, calls=%fused_computation.9.clone.1 | custom fusion | flops 4096 | bytes 65536 | tf_op jit(solution)/shard_map/while/body/scatter-add | solution.py:109
  1229.1 23.0 %gather_fusion.2 = f32[4096]{0:T(1024)S(1)} fusion(f32[3072]{0:T(1024)S(1)} %get-tuple-element.689, s32[4096]{0:T(1024)S(1)} %broadcast_clamp_fusion.9), kind=kCustom, calls=%fused_computation.2.clone.1 | custom fusion | bytes 49152 | tf_op jit(solution)/shard_map/while/body/gather | solution.py:35
  1254.0 22.4 %scatter_fusion.2 = f32[3072]{0:T(1024)S(1)} fusion(f32[3072]{0:T(1024)S(1)} %get-tuple-element.672, s32[4096]{0:T(1024)S(1)} %bitcast.291, f32[4096]{0:T(1024)S(1)} %bitcast.288), kind=kCustom, calls=%fused_computation.9.clone.1 | custom fusion | flops 4096 | bytes 65536 | tf_op jit(solution)/shard_map/while/body/scatter-add | solution.py:109
  1277.1 23.0 %gather_fusion.2 = f32[4096]{0:T(1024)S(1)} fusion(f32[3072]{0:T(1024)S(1)} %get-tuple-element.689, s32[4096]{0:T(1024)S(1)} %broadcast_clamp_fusion.9), kind=kCustom, calls=%fused_computation.2.clone.1 | custom fusion | bytes 49152 | tf_op jit(solution)/shard_map/while/body/gather | solution.py:35
  1302.0 22.4 %scatter_fusion.2 = f32[3072]{0:T(1024)S(1)} fusion(f32[3072]{0:T(1024)S(1)} %get-tuple-element.672, s32[4096]{0:T(1024)S(1)} %bitcast.291, f32[4096]{0:T(1024)S(1)} %bitcast.288), kind=kCustom, calls=%fused_computation.9.clone.1 | custom fusion | flops 4096 | bytes 65536 | tf_op jit(solution)/shard_map/while/body/scatter-add | solution.py:109
  1325.1 1.9 collective-permute-start.21
  1327.0 48.9 %collective-permute-start.20 = (f32[1,3,256]{2,1,0:T(4,128)S(1)}, f32[1,3,256]{2,1,0:T(4,128)S(1)}, u32[]{:S(2)}, u32[]{:S(2)}) collective-permute-start(f32[1,3,256]{2,1,0:T(4,128)S(1)} %get-tuple-element.345), channel_id=1, source_target_pairs={{32,0},{64,32},{96,64},{128,96},{160,128},{192,160},{224,192},{33,... | collective-permute-start | bytes 9224 | tf_op jit(solution)/shard_map/ppermute | solution.py:22
  1379.4 53.7 %collective-permute-done.22 = f32[5,1,256]{2,1,0:T(1,128)S(1)} collective-permute-done((f32[5,1,256]{2,1,0:T(1,128)S(1)}, f32[5,1,256]{2,1,0:T(1,128)S(1)}, u32[]{:S(2)}, u32[]{:S(2)}) %collective-permute-start.22) | collective-permute-done | bytes 5152 | tf_op jit(solution)/shard_map/ppermute | solution.py:22
  1433.1 6.1 scatter_fusion.5
  1439.8 216.6 %psum.47 = f32[]{:T(128)} all-reduce(f32[]{:T(128)} %multiply_reduce_fusion.12), channel_id=1, replica_groups=mesh['row'=8,'col'=32] {'row','col'}, use_global_device_ids=true, to_apply=%region_35.0 | all-reduce | flops 1 | bytes 8 | tf_op jit(solution)/shard_map/psum | solution.py:144
  1657.8 2.2 gather_fusion.6
  1660.1 1.9 stack.176
  1661.9 6.4 all-to-all-start
  1668.4 76.4 %all-to-all-done = f32[256,7,320]{2,1,0:T(8,128)S(1)} async-done(((f32[256,7,320]{2,1,0:T(8,128)}), f32[256,7,320]{2,1,0:T(8,128)S(1)}, u32[]{:S(2)}, u32[]{:S(2)}) %all-to-all-start) | async-done | bytes 2293792 | tf_op jit(solution)/shard_map/all_to_all | solution.py:161
  1744.8 2.1 copy.14
  1746.9 3.1 reshape.49
  1750.0 16.1 while.47
  (296 shorter events, 50.1 us)
Async XLA Ops:
  0.6 0.8 copy-start
  0.6 24.5 %copy-start.2 = (s32[4,8192]{1,0:T(4,128)S(1)}, s32[4,8192]{1,0:T(4,128)}, u32[]{:S(2)}) copy-start(s32[4,8192]{1,0:T(4,128)} %param.20) | copy-start | bytes 393220
  7.6 6.4 collective-permute-start
  12.1 4.9 collective-permute-start.1
  17.1 4.9 collective-permute-start.2
  20.6 4.6 collective-permute-start.3
  25.2 195.3 %copy-start.3 = (f32[2048]{0:T(1024)S(1)}, f32[2048]{0:T(1024)}, u32[]{:S(2)}) copy-start(f32[2048]{0:T(1024)} %param.26) | copy-start | bytes 24580
  169.8 50.6 %collective-permute-start.5 = (f32[1,3,256]{2,1,0:T(4,128)S(1)}, f32[1,3,256]{2,1,0:T(4,128)S(1)}, u32[]{:S(2)}, u32[]{:S(2)}) collective-permute-start(f32[1,3,256]{2,1,0:T(4,128)S(1)} %get-tuple-element.354), channel_id=1, source_target_pairs={{0,32},{32,64},{64,96},{96,128},{128,160},{160,192},{192,224},{1,3... | collective-permute-start | bytes 9224 | tf_op jit(solution)/shard_map/ppermute | solution.py:19
  171.7 49.5 %collective-permute-start.4 = (f32[1,3,256]{2,1,0:T(4,128)S(1)}, f32[1,3,256]{2,1,0:T(4,128)S(1)}, u32[]{:S(2)}, u32[]{:S(2)}) collective-permute-start(f32[1,3,256]{2,1,0:T(4,128)S(1)} %get-tuple-element.353), channel_id=1, source_target_pairs={{32,0},{64,32},{96,64},{128,96},{160,128},{192,160},{224,192},{33,... | collective-permute-start | bytes 9224 | tf_op jit(solution)/shard_map/ppermute | solution.py:22
  221.3 2.6 collective-permute-start.7
  222.5 59.4 %collective-permute-start.6 = (f32[5,1,256]{2,1,0:T(1,128)S(1)}, f32[5,1,256]{2,1,0:T(1,128)S(1)}, u32[]{:S(2)}, u32[]{:S(2)}) collective-permute-start(f32[5,1,256]{2,1,0:T(1,128)S(1)} %get-tuple-element.315), channel_id=1, source_target_pairs={{1,0},{2,1},{3,2},{4,3},{5,4},{6,5},{7,6},{8,7},{9,8},{10,9},{11,1... | collective-permute-start | bytes 15368 | tf_op jit(solution)/shard_map/ppermute | solution.py:22
  288.1 304.7 %copy-start.5 = (f32[320]{0:T(512)S(1)}, f32[320]{0:T(512)}, u32[]{:S(2)}) copy-start(f32[320]{0:T(512)} %param.29) | copy-start | bytes 3844
  288.1 304.7 %copy-start.8 = (f32[320]{0:T(512)S(1)}, f32[320]{0:T(512)}, u32[]{:S(2)}) copy-start(f32[320]{0:T(512)} %param.30) | copy-start | bytes 3844
  589.5 5.3 collective-permute-start.8
  592.9 4.9 collective-permute-start.9
  597.8 5.0 collective-permute-start.10
  601.5 4.4 collective-permute-start.11
  750.5 50.8 %collective-permute-start.13 = (f32[1,3,256]{2,1,0:T(4,128)S(1)}, f32[1,3,256]{2,1,0:T(4,128)S(1)}, u32[]{:S(2)}, u32[]{:S(2)}) collective-permute-start(f32[1,3,256]{2,1,0:T(4,128)S(1)} %get-tuple-element.350), channel_id=1, source_target_pairs={{0,32},{32,64},{64,96},{96,128},{128,160},{160,192},{192,224},{1,3... | collective-permute-start | bytes 9224 | tf_op jit(solution)/shard_map/ppermute | solution.py:19
  752.4 49.7 %collective-permute-start.12 = (f32[1,3,256]{2,1,0:T(4,128)S(1)}, f32[1,3,256]{2,1,0:T(4,128)S(1)}, u32[]{:S(2)}, u32[]{:S(2)}) collective-permute-start(f32[1,3,256]{2,1,0:T(4,128)S(1)} %get-tuple-element.349), channel_id=1, source_target_pairs={{32,0},{64,32},{96,64},{128,96},{160,128},{192,160},{224,192},{33,... | collective-permute-start | bytes 9224 | tf_op jit(solution)/shard_map/ppermute | solution.py:22
  802.1 2.6 collective-permute-start.15
  803.4 55.0 %collective-permute-start.14 = (f32[5,1,256]{2,1,0:T(1,128)S(1)}, f32[5,1,256]{2,1,0:T(1,128)S(1)}, u32[]{:S(2)}, u32[]{:S(2)}) collective-permute-start(f32[5,1,256]{2,1,0:T(1,128)S(1)} %get-tuple-element.311), channel_id=1, source_target_pairs={{1,0},{2,1},{3,2},{4,3},{5,4},{6,5},{7,6},{8,7},{9,8},{10,9},{11,1... | collective-permute-start | bytes 15368 | tf_op jit(solution)/shard_map/ppermute | solution.py:22
  858.5 225.3 %copy-start.6 = (f32[320]{0:T(512)S(1)}, f32[320]{0:T(512)}, u32[]{:S(2)}) copy-start(f32[320]{0:T(512)} %param.31) | copy-start | bytes 3844
  864.6 302.8 %copy-start.7 = (s32[320]{0:T(512)S(1)}, s32[320]{0:T(512)}, u32[]{:S(2)}) copy-start(s32[320]{0:T(512)} %param.27) | copy-start | bytes 3844
  1164.4 5.0 collective-permute-start.16
  1167.4 4.9 collective-permute-start.17
  1172.4 5.0 collective-permute-start.18
  1176.1 4.4 collective-permute-start.19
  1325.1 50.8 %collective-permute-start.21 = (f32[1,3,256]{2,1,0:T(4,128)S(1)}, f32[1,3,256]{2,1,0:T(4,128)S(1)}, u32[]{:S(2)}, u32[]{:S(2)}) collective-permute-start(f32[1,3,256]{2,1,0:T(4,128)S(1)} %get-tuple-element.346), channel_id=1, source_target_pairs={{0,32},{32,64},{64,96},{96,128},{128,160},{160,192},{192,224},{1,3... | collective-permute-start | bytes 9224 | tf_op jit(solution)/shard_map/ppermute | solution.py:19
  1327.0 49.7 %collective-permute-start.20 = (f32[1,3,256]{2,1,0:T(4,128)S(1)}, f32[1,3,256]{2,1,0:T(4,128)S(1)}, u32[]{:S(2)}, u32[]{:S(2)}) collective-permute-start(f32[1,3,256]{2,1,0:T(4,128)S(1)} %get-tuple-element.345), channel_id=1, source_target_pairs={{32,0},{64,32},{96,64},{128,96},{160,128},{192,160},{224,192},{33,... | collective-permute-start | bytes 9224 | tf_op jit(solution)/shard_map/ppermute | solution.py:22
  1376.7 2.6 collective-permute-start.23
  1378.0 55.0 %collective-permute-start.22 = (f32[5,1,256]{2,1,0:T(1,128)S(1)}, f32[5,1,256]{2,1,0:T(1,128)S(1)}, u32[]{:S(2)}, u32[]{:S(2)}) collective-permute-start(f32[5,1,256]{2,1,0:T(1,128)S(1)} %get-tuple-element.307), channel_id=1, source_target_pairs={{1,0},{2,1},{3,2},{4,3},{5,4},{6,5},{7,6},{8,7},{9,8},{10,9},{11,1... | collective-permute-start | bytes 15368 | tf_op jit(solution)/shard_map/ppermute | solution.py:22
  1433.1 227.0 %copy-start.4 = (f32[3,320]{1,0:T(4,128)S(1)}, f32[3,320]{1,0:T(4,128)}, u32[]{:S(2)}) copy-start(f32[3,320]{1,0:T(4,128)} %param.28) | copy-start | bytes 11524
  1657.8 4.2 copy-start.1
  1661.9 82.9 %all-to-all-start = ((f32[256,7,320]{2,1,0:T(8,128)}), f32[256,7,320]{2,1,0:T(8,128)S(1)}, u32[]{:S(2)}, u32[]{:S(2)}) async-start(f32[256,7,320]{2,1,0:T(8,128)} %stack.176), calls=%async_computation | async-start | bytes 6291456 | tf_op jit(solution)/shard_map/all_to_all | solution.py:161
  1746.9 3.1 slice-start
